TPU v7x, 32 devices: a whole 2x2x4 slice. The times are simulated.
32 devices in a mesh: pole: 4 (over y, x), row: 8 (over z, core).
Axes of the slice: x: 2, y: 2, z: 4, core: 2. Of those that a mesh axis runs over, the one named last changes fastest.
Arguments:
- basis: bfloat16 [32768, 128], P('row'), may hold values from -24 to 24
- inverses: bfloat16 [4, 64, 512, 512], P('pole', 'row'), may hold values from -1.5 to 1.5
- lower: bfloat16 [64, 512, 512], P('row'), may hold values from -0.03955078 to 0.03955078
- upper: bfloat16 [64, 512, 512], P('row'), may hold values from -0.03955078 to 0.03955078
- pole_weights: float32 [4], P('pole'), may hold values from 0.5 to 1.5
Outputs:
- new_basis: float32 [32768, 128], P(('row', 'pole'))
All inputs are finite; a program needn't handle non-finite values.
Results may differ from a plain program's by a relative error of at most 0.003.
Values may be sent and summed in bfloat16 or wider, within the bound.
A program may use at most 64 MiB of HBM per device.

v0:
```python
import jax
import jax.numpy as jnp
from jax import lax
from jax.sharding import PartitionSpec as P

SWEEPS = 4


def padded_2(value, sides, width):
    for axis, dim in sides:
        peers, length = (lax.axis_size(axis), value.shape[dim])
        up = [(i, (i + 1) % peers) for i in range(peers - 1)]
        down = [(j, i) for i, j in up]
        last = lax.slice_in_dim(value, length - width, length, axis=dim)
        initial = lax.slice_in_dim(value, 0, width, axis=dim)
        before = lax.ppermute(last, axis, up)
        after = lax.ppermute(initial, axis, down)
        value = jnp.concatenate([before, value, after], axis=dim)
    return value


def shards(basis, inverses, lower, upper, pole_weights):
    rows, width = basis.shape
    count = inverses.shape[1]
    size = inverses.shape[-1]
    inverse = inverses[0]
    blocks = basis.reshape(count, size, width)
    state = jnp.einsum("bij,bjk->bik", inverse, blocks, preferred_element_type=jnp.float32).astype(
        jnp.bfloat16
    )
    for sweep in range(SWEEPS):
        padded = padded_2(state.reshape(rows, width), (("row", 0),), size)
        padded = padded.reshape(count + 2, size, width)
        rhs = blocks.astype(jnp.float32)
        rhs = rhs + jnp.einsum(
            "bij,bjk->bik", lower, padded[:-2], preferred_element_type=jnp.float32
        )
        rhs = rhs + jnp.einsum(
            "bij,bjk->bik", upper, padded[2:], preferred_element_type=jnp.float32
        )
        state = jnp.einsum(
            "bij,bjk->bik", inverse, rhs.astype(jnp.bfloat16), preferred_element_type=jnp.float32
        ).astype(jnp.bfloat16)
    weighted = pole_weights[0] * state.reshape(rows, width).astype(jnp.float32)
    total_rows = rows * lax.axis_size("row")
    filtered = lax.psum(weighted, "pole")
    share = rows // lax.axis_size("pole")
    mine = lax.dynamic_slice_in_dim(filtered, lax.axis_index("pole") * share, share, 0)
    partial_gram = jnp.dot(filtered.T, filtered, precision=lax.Precision.HIGHEST)
    gram = lax.psum(partial_gram, "row")
    gram = gram / total_rows
    factor = jnp.linalg.cholesky(gram)
    solved = jax.scipy.linalg.solve_triangular(factor, mine.T, lower=True)
    return solved.T


def solution(mesh):
    return jax.shard_map(
        shards,
        mesh=mesh,
        in_specs=(
            P("row", None),
            P("pole", "row", None, None),
            P("row", None, None),
            P("row", None, None),
            P("pole"),
        ),
        out_specs=P(("row", "pole"), None),
        check_vma=False,
    )
```

profile of v0, /device:TPU:0, one launch (start us, length us, event | category | flops | bytes accessed | tf_op | source)
XLA Modules:
  0.0 268.5 jit_solution(1977090597358284194)
XLA Ops:
  6.5 3.8 %fusion.18 = bf16[8,512,128]{2,1,0:T(8,128)(2,1)S(1)} fusion(bf16[8,512,128]{2,1,0:T(8,128)(2,1)} %bitcast.142, bf16[1,8,512,512]{3,2,1,0:T(8,128)(2,1)} %param.6), kind=kOutput, calls=%fused_computation.23 | convolution fusion | flops 537395200 | bytes 6291456 | tf_op jit(solution)/shard_map/bij,bjk->bik/dot_general | solution.py:28
  10.4 2.4 collective-permute-start
  12.8 1.3 collective-permute-start.1
  14.7 3.7 %collective-permute-done.1 = bf16[512,128]{1,0:T(8,128)(2,1)} collective-permute-done((bf16[512,128]{1,0:T(8,128)(2,1)S(1)}, bf16[512,128]{1,0:T(8,128)(2,1)}, u32[]{:S(2)}, u32[]{:S(2)}) %collective-permute-start.1) | collective-permute-done | bytes 131104 | tf_op jit(solution)/shard_map/ppermute | solution.py:17
  18.4 2.0 pad_maximum_fusion.6
  20.4 3.7 %fusion.50 = f32[8,128,512]{2,1,0:T(8,128)S(1)} fusion(bf16[8,512,128]{2,1,0:T(8,128)(2,1)S(1)} %bitcast.131, bf16[8,512,512]{2,1,0:T(8,128)(2,1)} %param.7), kind=kOutput, calls=%fused_computation.60 | convolution fusion | flops 536870912 | bytes 7340032 | tf_op jit(solution)/shard_map/bij,bjk->bik/dot_general | solution.py:35
  24.1 7.6 %fusion.41 = bf16[8,512,128]{1,2,0:T(8,128)(2,1)} fusion(bf16[1,8,512,512]{3,2,1,0:T(8,128)(2,1)} %param.6, bf16[8,512,128]{1,2,0:T(8,128)(2,1)S(1)} %copy.15, f32[8,128,512]{2,1,0:T(8,128)S(1)} %fusion.50, bf16[8,512,128]{2,1,0:T(8,128)(2,1)} %bitcast.138, bf16[8,512,512]{2,1,0:T(8,128)(2,1)} %param.8), kind=kOutput, calls=%fused_computation.30 | convolution fusion | flops 1076363264 | bytes 13631488 | tf_op jit(solution)/shard_map/bij,bjk->bik/dot_general | solution.py:41
  32.7 5.4 %collective-permute-start.2 = (bf16[512,128]{0,1:T(8,128)(2,1)S(1)}, bf16[512,128]{0,1:T(8,128)(2,1)S(1)}, u32[]{:S(2)}, u32[]{:S(2)}) collective-permute-start(bf16[512,128]{0,1:T(8,128)(2,1)S(1)} %get-tuple-element.16), channel_id=1, source_target_pairs={{0,1},{1,2},{2,3},{3,4},{4,5},{5,6},{6,7},{8,9},{9,10},{10,11},{11... | collective-permute-start | bytes 393224 | tf_op jit(solution)/shard_map/ppermute | solution.py:16
  38.1 1.3 collective-permute-start.3
  39.4 1.6 copy.16
  41.5 1.1 pad_maximum_fusion.4
  42.6 3.7 %fusion.51 = f32[8,128,512]{2,1,0:T(8,128)S(1)} fusion(bf16[8,512,128]{2,1,0:T(8,128)(2,1)S(1)} %bitcast.132, bf16[8,512,512]{2,1,0:T(8,128)(2,1)} %param.7), kind=kOutput, calls=%fused_computation.61 | convolution fusion | flops 536870912 | bytes 7340032 | tf_op jit(solution)/shard_map/bij,bjk->bik/dot_general | solution.py:35
  46.3 7.6 %fusion.38 = bf16[8,512,128]{1,2,0:T(8,128)(2,1)} fusion(bf16[1,8,512,512]{3,2,1,0:T(8,128)(2,1)} %param.6, bf16[8,512,128]{1,2,0:T(8,128)(2,1)S(1)} %copy.15, f32[8,128,512]{2,1,0:T(8,128)S(1)} %fusion.51, bf16[8,512,128]{2,1,0:T(8,128)(2,1)} %bitcast.139, bf16[8,512,512]{2,1,0:T(8,128)(2,1)} %param.8), kind=kOutput, calls=%fused_computation.29 | convolution fusion | flops 1076363264 | bytes 13631488 | tf_op jit(solution)/shard_map/bij,bjk->bik/dot_general | solution.py:41
  55.0 5.0 %collective-permute-start.4 = (bf16[512,128]{0,1:T(8,128)(2,1)S(1)}, bf16[512,128]{0,1:T(8,128)(2,1)S(1)}, u32[]{:S(2)}, u32[]{:S(2)}) collective-permute-start(bf16[512,128]{0,1:T(8,128)(2,1)S(1)} %get-tuple-element.12), channel_id=1, source_target_pairs={{0,1},{1,2},{2,3},{3,4},{4,5},{5,6},{6,7},{8,9},{9,10},{10,11},{11... | collective-permute-start | bytes 393224 | tf_op jit(solution)/shard_map/ppermute | solution.py:16
  59.9 1.3 collective-permute-start.5
  61.2 1.6 copy.19
  63.3 1.1 pad_maximum_fusion.2
  64.4 3.7 %fusion.52 = f32[8,128,512]{2,1,0:T(8,128)S(1)} fusion(bf16[8,512,128]{2,1,0:T(8,128)(2,1)S(1)} %bitcast.133, bf16[8,512,512]{2,1,0:T(8,128)(2,1)} %param.7), kind=kOutput, calls=%fused_computation.62 | convolution fusion | flops 536870912 | bytes 7340032 | tf_op jit(solution)/shard_map/bij,bjk->bik/dot_general | solution.py:35
  68.1 7.6 %fusion.35 = bf16[8,512,128]{1,2,0:T(8,128)(2,1)} fusion(bf16[1,8,512,512]{3,2,1,0:T(8,128)(2,1)} %param.6, bf16[8,512,128]{1,2,0:T(8,128)(2,1)S(1)} %copy.15, f32[8,128,512]{2,1,0:T(8,128)S(1)} %fusion.52, bf16[8,512,128]{2,1,0:T(8,128)(2,1)} %bitcast.140, bf16[8,512,512]{2,1,0:T(8,128)(2,1)} %param.8), kind=kOutput, calls=%fused_computation.28 | convolution fusion | flops 1076363264 | bytes 13631488 | tf_op jit(solution)/shard_map/bij,bjk->bik/dot_general | solution.py:41
  76.7 5.0 %collective-permute-start.6 = (bf16[512,128]{0,1:T(8,128)(2,1)S(1)}, bf16[512,128]{0,1:T(8,128)(2,1)S(1)}, u32[]{:S(2)}, u32[]{:S(2)}) collective-permute-start(bf16[512,128]{0,1:T(8,128)(2,1)S(1)} %get-tuple-element.8), channel_id=1, source_target_pairs={{0,1},{1,2},{2,3},{3,4},{4,5},{5,6},{6,7},{8,9},{9,10},{10,11},{11... | collective-permute-start | bytes 393224 | tf_op jit(solution)/shard_map/ppermute | solution.py:16
  81.7 1.5 collective-permute-start.7
  83.8 1.6 copy.22
  85.7 1.1 pad_maximum_fusion
  86.9 3.7 %fusion.53 = f32[8,128,512]{2,1,0:T(8,128)S(1)} fusion(bf16[8,512,128]{2,1,0:T(8,128)(2,1)S(1)} %bitcast.134, bf16[8,512,512]{2,1,0:T(8,128)(2,1)} %param.7), kind=kOutput, calls=%fused_computation.63 | convolution fusion | flops 536870912 | bytes 7340032 | tf_op jit(solution)/shard_map/bij,bjk->bik/dot_general | solution.py:35
  90.6 8.0 %multiply_bitcast_fusion = f32[8,512,128]{1,2,0:T(8,128)} fusion(bf16[1,8,512,512]{3,2,1,0:T(8,128)(2,1)} %param.6, bf16[8,512,128]{1,2,0:T(8,128)(2,1)S(1)} %copy.15, f32[8,128,512]{2,1,0:T(8,128)S(1)} %fusion.53, bf16[8,512,128]{2,1,0:T(8,128)(2,1)} %bitcast.130, bf16[8,512,512]{2,1,0:T(8,128)(2,1)} %param.8, f32[]{:T(128)} %bitcast.128), kind=kOutput, calls=%fused_computation.22 | convolution fusion | flops 1077411840 | bytes 14680068 | tf_op jit(solution)/shard_map/bij,bjk->bik/dot_general | solution.py:41
  98.5 2.9 %copy.25 = f32[8,512,128]{2,1,0:T(8,128)} copy(f32[8,512,128]{1,2,0:T(8,128)} %multiply_bitcast_fusion) | data formatting | bytes 4194304 | tf_op jit(solution)/shard_map/mul | solution.py:44
  101.5 71.8 %all-reduce.3.cloned.1.call-done = f32[4096,128]{1,0:T(8,128)} async-done(((f32[4096,128]{1,0:T(8,128)}), f32[4096,128]{1,0:T(8,128)}) %all-reduce.3.cloned.1.call-update) | async-done | bytes 2097168 | tf_op jit(solution)/shard_map/psum | solution.py:46
  173.4 6.3 %fusion.54 = f32[128,128]{0,1:T(8,128)} fusion(f32[4096,128]{1,0:T(8,128)} %all-reduce.3.cloned.1.call-done), kind=kOutput, calls=%fused_computation.64 | convolution fusion | flops 805306368 | bytes 2162688 | tf_op jit(solution)/shard_map/dot_general | solution.py:49
  179.7 54.8 %all-reduce.5.cloned.1.call-done = f32[128,128]{0,1:T(8,128)} async-done(((f32[128,128]{0,1:T(8,128)}), f32[128,128]{0,1:T(8,128)}) %all-reduce.5.cloned.1.call-update) | async-done | bytes 65552 | tf_op jit(solution)/shard_map/psum | solution.py:50
  236.3 11.7 %cholesky.16 = f32[128,128]{1,0:T(8,128)S(1)} custom-call(f32[128,128]{1,0:T(8,128)S(1)} %fusion.48), custom_call_target="Cholesky" | custom-call | tf_op jit(solution)/shard_map/jit(cholesky)/cholesky | solution.py:52
  249.4 9.8 %custom-call.7 = f32[1,128,128]{1,2,0:T(8,128)S(1)} custom-call(f32[1,128,128]{2,1,0:T(8,128)S(1)} %fusion.46), custom_call_target="InvertDiagBlocksLowerTriangular" | custom-call | tf_op jit(solution)/shard_map/jit(_solve_triangular)/triangular_solve | solution.py:53
  259.2 2.4 fusion.44
  (30 shorter events, 7.8 us)
Async XLA Ops:
  6.5 166.8 %all-reduce.3.cloned.1.call-start = ((), (), s32[]{:S(2)}) async-start(), calls=%async_computation | async-start | bytes 4194304 | tf_op jit(solution)/shard_map/psum | solution.py:46
  6.5 7.6 %copy-start = (bf16[4096,128]{1,0:T(8,128)(2,1)S(1)}, bf16[4096,128]{1,0:T(8,128)(2,1)}, u32[]{:S(2)}) copy-start(bf16[4096,128]{1,0:T(8,128)(2,1)} %param.5) | copy-start | bytes 3145732
  10.4 4.3 %collective-permute-start = (bf16[512,128]{1,0:T(8,128)(2,1)S(1)}, bf16[512,128]{1,0:T(8,128)(2,1)S(1)}, u32[]{:S(2)}, u32[]{:S(2)}) collective-permute-start(bf16[512,128]{1,0:T(8,128)(2,1)S(1)} %get-tuple-element.20), channel_id=1, source_target_pairs={{0,1},{1,2},{2,3},{3,4},{4,5},{5,6},{6,7},{8,9},{9,10},{10,11},{11... | collective-permute-start | bytes 393224 | tf_op jit(solution)/shard_map/ppermute | solution.py:16
  12.8 5.5 %collective-permute-start.1 = (bf16[512,128]{1,0:T(8,128)(2,1)S(1)}, bf16[512,128]{1,0:T(8,128)(2,1)}, u32[]{:S(2)}, u32[]{:S(2)}) collective-permute-start(bf16[512,128]{1,0:T(8,128)(2,1)S(1)} %get-tuple-element.19), channel_id=1, source_target_pairs={{1,0},{2,1},{3,2},{4,3},{5,4},{6,5},{7,6},{9,8},{10,9},{11,10},{12... | collective-permute-start | bytes 393224 | tf_op jit(solution)/shard_map/ppermute | solution.py:17
  32.7 8.4 %collective-permute-start.2 = (bf16[512,128]{0,1:T(8,128)(2,1)S(1)}, bf16[512,128]{0,1:T(8,128)(2,1)S(1)}, u32[]{:S(2)}, u32[]{:S(2)}) collective-permute-start(bf16[512,128]{0,1:T(8,128)(2,1)S(1)} %get-tuple-element.16), channel_id=1, source_target_pairs={{0,1},{1,2},{2,3},{3,4},{4,5},{5,6},{6,7},{8,9},{9,10},{10,11},{11... | collective-permute-start | bytes 393224 | tf_op jit(solution)/shard_map/ppermute | solution.py:16
  38.1 3.2 %collective-permute-start.3 = (bf16[512,128]{0,1:T(8,128)(2,1)S(1)}, bf16[512,128]{0,1:T(8,128)(2,1)S(1)}, u32[]{:S(2)}, u32[]{:S(2)}) collective-permute-start(bf16[512,128]{0,1:T(8,128)(2,1)S(1)} %get-tuple-element.15), channel_id=1, source_target_pairs={{1,0},{2,1},{3,2},{4,3},{5,4},{6,5},{7,6},{9,8},{10,9},{11,10},{12... | collective-permute-start | bytes 393224 | tf_op jit(solution)/shard_map/ppermute | solution.py:17
  55.0 7.9 %collective-permute-start.4 = (bf16[512,128]{0,1:T(8,128)(2,1)S(1)}, bf16[512,128]{0,1:T(8,128)(2,1)S(1)}, u32[]{:S(2)}, u32[]{:S(2)}) collective-permute-start(bf16[512,128]{0,1:T(8,128)(2,1)S(1)} %get-tuple-element.12), channel_id=1, source_target_pairs={{0,1},{1,2},{2,3},{3,4},{4,5},{5,6},{6,7},{8,9},{9,10},{10,11},{11... | collective-permute-start | bytes 393224 | tf_op jit(solution)/shard_map/ppermute | solution.py:16
  59.9 3.2 %collective-permute-start.5 = (bf16[512,128]{0,1:T(8,128)(2,1)S(1)}, bf16[512,128]{0,1:T(8,128)(2,1)S(1)}, u32[]{:S(2)}, u32[]{:S(2)}) collective-permute-start(bf16[512,128]{0,1:T(8,128)(2,1)S(1)} %get-tuple-element.11), channel_id=1, source_target_pairs={{1,0},{2,1},{3,2},{4,3},{5,4},{6,5},{7,6},{9,8},{10,9},{11,10},{12... | collective-permute-start | bytes 393224 | tf_op jit(solution)/shard_map/ppermute | solution.py:17
  76.7 8.7 %collective-permute-start.6 = (bf16[512,128]{0,1:T(8,128)(2,1)S(1)}, bf16[512,128]{0,1:T(8,128)(2,1)S(1)}, u32[]{:S(2)}, u32[]{:S(2)}) collective-permute-start(bf16[512,128]{0,1:T(8,128)(2,1)S(1)} %get-tuple-element.8), channel_id=1, source_target_pairs={{0,1},{1,2},{2,3},{3,4},{4,5},{5,6},{6,7},{8,9},{9,10},{10,11},{11... | collective-permute-start | bytes 393224 | tf_op jit(solution)/shard_map/ppermute | solution.py:16
  81.7 3.9 %collective-permute-start.7 = (bf16[512,128]{0,1:T(8,128)(2,1)S(1)}, bf16[512,128]{0,1:T(8,128)(2,1)S(1)}, u32[]{:S(2)}, u32[]{:S(2)}) collective-permute-start(bf16[512,128]{0,1:T(8,128)(2,1)S(1)} %get-tuple-element.7), channel_id=1, source_target_pairs={{1,0},{2,1},{3,2},{4,3},{5,4},{6,5},{7,6},{9,8},{10,9},{11,10},{12... | collective-permute-start | bytes 393224 | tf_op jit(solution)/shard_map/ppermute | solution.py:17
  101.5 133.1 %all-reduce.5.cloned.1.call-start = ((), (), s32[]{:S(2)}) async-start(), calls=%async_computation.1 | async-start | bytes 131072 | tf_op jit(solution)/shard_map/psum | solution.py:50
Sparse Core Ops, SparseCore 0:
  101.6 71.7 all-reduce.2
  179.8 54.6 all-reduce.4
where the time goes:
time: 269 us; the launch traced here: 268 us
  waiting for transfers between devices  131 us (49%)
  matrix products  58.2 us (22%)
  other arithmetic  29.9 us (11%)
  starting transfers between devices  23.2 us (9%)
  between operations  14.3 us (5%)
  local copies, waits for them, and re-layouts  12.1 us (4%)
    psum x1, waiting for transfers between devices, shards(): filtered = lax.psum(weighted, 'pole')  71.8 us
    psum x1, waiting for transfers between devices, shards(): gram = lax.psum(partial_gram, 'row')  54.8 us
    dot_general x4, matrix products, shards(): jnp.einsum('bij,bjk->bik', inverse, rhs.astype(jnp.bfloat16), preferred_e...  30.9 us
    ppermute x4, starting transfers between devices, padded_2(): before = lax.ppermute(last, axis, up)  17.8 us
    dot_general x4, matrix products, shards(): jnp.einsum('bij,bjk->bik', lower, padded[:-2], preferred_element_type=jnp...  14.8 us
    another operation x3, other arithmetic, shards(): factor = jnp.linalg.cholesky(gram)  12.4 us
    another operation x2, other arithmetic, shards(): solved = jax.scipy.linalg.solve_triangular(factor, mine.T, lower=True)  10.5 us
    dot_general x1, matrix products, shards(): jnp.dot(filtered.T, filtered, precision=lax.Precision.HIGHEST)  6.31 us
  transfers between devices with their start and end apart: 10, of which 5 were waited for; matrix products, arithmetic and copies ran while one was open for 2% of the time, Pallas kernels for 0%

commit v1 on v0

--- a/solution.py
+++ b/solution.py
@@ -1,9 +1,17 @@
+import functools
 import jax
 import jax.numpy as jnp
 from jax import lax
 from jax.sharding import PartitionSpec as P
 
 SWEEPS = 4
+
+
+def direct_node_for(body, shard_axis):
+    return jnp.sum(jax.lax.all_gather(body, shard_axis), 0)
+
+
+manage_islands = functools.partial(direct_node_for, shard_axis="row")
 
 
 def padded_2(value, sides, width):
@@ -47,7 +55,7 @@
     share = rows // lax.axis_size("pole")
     mine = lax.dynamic_slice_in_dim(filtered, lax.axis_index("pole") * share, share, 0)
     partial_gram = jnp.dot(filtered.T, filtered, precision=lax.Precision.HIGHEST)
-    gram = lax.psum(partial_gram, "row")
+    gram = manage_islands(partial_gram)
     gram = gram / total_rows
     factor = jnp.linalg.cholesky(gram)
     solved = jax.scipy.linalg.solve_triangular(factor, mine.T, lower=True)

time: 269 us -> 227 us (0.84)
  waiting for transfers between devices: 131 us -> 76 us
  blocking collectives: 0 us -> 15 us
    psum x1 -> x0, waiting for transfers between devices: 54.8 us -> none  [shards(): gram = lax.psum(partial_gram, 'row')]
    all_gather x0 -> x1, blocking collectives: none -> 15 us  [direct_node_for(): return jnp.sum(jax.lax.all_gather(body, shard_axis), 0)]
  transfers between devices with their start and end apart: 10 -> 9, of which waited for: 5 -> 4; matrix products, arithmetic and copies ran while one was open for 2% -> 3% of each run, Pallas kernels for 0% -> 0%
where the time goes in v1:
time: 227 us; the launch traced here: 226 us
  waiting for transfers between devices  76 us (33%)
  matrix products  57.6 us (25%)
  other arithmetic  28.2 us (12%)
  starting transfers between devices  23.1 us (10%)
  blocking collectives  15 us (7%)
  between operations  14.3 us (6%)
  local copies, waits for them, and re-layouts  12 us (5%)
    psum x1, waiting for transfers between devices, shards(): filtered = lax.psum(weighted, 'pole')  71.9 us
    dot_general x4, matrix products, shards(): jnp.einsum('bij,bjk->bik', inverse, rhs.astype(jnp.bfloat16), preferred_e...  31 us
    ppermute x4, starting transfers between devices, padded_2(): before = lax.ppermute(last, axis, up)  17.8 us
    all_gather x1, blocking collectives, direct_node_for(): return jnp.sum(jax.lax.all_gather(body, shard_axis), 0)  15 us
    dot_general x4, matrix products, shards(): jnp.einsum('bij,bjk->bik', lower, padded[:-2], preferred_element_type=jnp...  14.8 us
    another operation x3, other arithmetic, shards(): factor = jnp.linalg.cholesky(gram)  12.4 us
    another operation x2, other arithmetic, shards(): solved = jax.scipy.linalg.solve_triangular(factor, mine.T, lower=True)  10.5 us
    dot_general x1, matrix products, shards(): jnp.dot(filtered.T, filtered, precision=lax.Precision.HIGHEST)  5.66 us
  transfers between devices with their start and end apart: 9, of which 4 were waited for; matrix products, arithmetic and copies ran while one was open for 3% of the time, Pallas kernels for 0%

profile of v1, /device:TPU:0, one launch (start us, length us, event | category | flops | bytes accessed | tf_op | source)
XLA Modules:
  0.0 226.3 jit_solution(10256084464301204904)
XLA Ops:
  6.5 3.8 %fusion.18 = bf16[8,512,128]{2,1,0:T(8,128)(2,1)S(1)} fusion(bf16[8,512,128]{2,1,0:T(8,128)(2,1)} %bitcast.144, bf16[1,8,512,512]{3,2,1,0:T(8,128)(2,1)} %param.6), kind=kOutput, calls=%fused_computation.23 | convolution fusion | flops 537395200 | bytes 6291456 | tf_op jit(solution)/shard_map/bij,bjk->bik/dot_general | solution.py:36
  10.4 2.4 %collective-permute-start = (bf16[512,128]{1,0:T(8,128)(2,1)S(1)}, bf16[512,128]{1,0:T(8,128)(2,1)S(1)}, u32[]{:S(2)}, u32[]{:S(2)}) collective-permute-start(bf16[512,128]{1,0:T(8,128)(2,1)S(1)} %get-tuple-element.20), channel_id=1, source_target_pairs={{0,1},{1,2},{2,3},{3,4},{4,5},{5,6},{6,7},{8,9},{9,10},{10,11},{11... | collective-permute-start | bytes 393224 | tf_op jit(solution)/shard_map/ppermute | solution.py:24
  12.8 1.3 collective-permute-start.1
  14.7 3.7 %collective-permute-done.1 = bf16[512,128]{1,0:T(8,128)(2,1)} collective-permute-done((bf16[512,128]{1,0:T(8,128)(2,1)S(1)}, bf16[512,128]{1,0:T(8,128)(2,1)}, u32[]{:S(2)}, u32[]{:S(2)}) %collective-permute-start.1) | collective-permute-done | bytes 131104 | tf_op jit(solution)/shard_map/ppermute | solution.py:25
  18.4 2.0 pad_maximum_fusion.6
  20.4 3.7 %fusion.50 = f32[8,128,512]{2,1,0:T(8,128)S(1)} fusion(bf16[8,512,128]{2,1,0:T(8,128)(2,1)S(1)} %bitcast.132, bf16[8,512,512]{2,1,0:T(8,128)(2,1)} %param.7), kind=kOutput, calls=%fused_computation.59 | convolution fusion | flops 536870912 | bytes 7340032 | tf_op jit(solution)/shard_map/bij,bjk->bik/dot_general | solution.py:43
  24.1 7.7 %fusion.41 = bf16[8,512,128]{1,2,0:T(8,128)(2,1)} fusion(bf16[1,8,512,512]{3,2,1,0:T(8,128)(2,1)} %param.6, bf16[8,512,128]{1,2,0:T(8,128)(2,1)S(1)} %copy.38, f32[8,128,512]{2,1,0:T(8,128)S(1)} %fusion.50, bf16[8,512,128]{2,1,0:T(8,128)(2,1)} %bitcast.139, bf16[8,512,512]{2,1,0:T(8,128)(2,1)} %param.8), kind=kOutput, calls=%fused_computation.30 | convolution fusion | flops 1076363264 | bytes 13631488 | tf_op jit(solution)/shard_map/bij,bjk->bik/dot_general | solution.py:49
  32.7 5.4 %collective-permute-start.2 = (bf16[512,128]{0,1:T(8,128)(2,1)S(1)}, bf16[512,128]{0,1:T(8,128)(2,1)S(1)}, u32[]{:S(2)}, u32[]{:S(2)}) collective-permute-start(bf16[512,128]{0,1:T(8,128)(2,1)S(1)} %get-tuple-element.16), channel_id=1, source_target_pairs={{0,1},{1,2},{2,3},{3,4},{4,5},{5,6},{6,7},{8,9},{9,10},{10,11},{11... | collective-permute-start | bytes 393224 | tf_op jit(solution)/shard_map/ppermute | solution.py:24
  38.2 1.3 collective-permute-start.3
  39.5 1.6 copy.41
  41.5 1.1 pad_maximum_fusion.4
  42.6 3.7 %fusion.51 = f32[8,128,512]{2,1,0:T(8,128)S(1)} fusion(bf16[8,512,128]{2,1,0:T(8,128)(2,1)S(1)} %bitcast.133, bf16[8,512,512]{2,1,0:T(8,128)(2,1)} %param.7), kind=kOutput, calls=%fused_computation.60 | convolution fusion | flops 536870912 | bytes 7340032 | tf_op jit(solution)/shard_map/bij,bjk->bik/dot_general | solution.py:43
  46.3 7.7 %fusion.38 = bf16[8,512,128]{1,2,0:T(8,128)(2,1)} fusion(bf16[1,8,512,512]{3,2,1,0:T(8,128)(2,1)} %param.6, bf16[8,512,128]{1,2,0:T(8,128)(2,1)S(1)} %copy.38, f32[8,128,512]{2,1,0:T(8,128)S(1)} %fusion.51, bf16[8,512,128]{2,1,0:T(8,128)(2,1)} %bitcast.140, bf16[8,512,512]{2,1,0:T(8,128)(2,1)} %param.8), kind=kOutput, calls=%fused_computation.29 | convolution fusion | flops 1076363264 | bytes 13631488 | tf_op jit(solution)/shard_map/bij,bjk->bik/dot_general | solution.py:49
  55.0 5.0 %collective-permute-start.4 = (bf16[512,128]{0,1:T(8,128)(2,1)S(1)}, bf16[512,128]{0,1:T(8,128)(2,1)S(1)}, u32[]{:S(2)}, u32[]{:S(2)}) collective-permute-start(bf16[512,128]{0,1:T(8,128)(2,1)S(1)} %get-tuple-element.12), channel_id=1, source_target_pairs={{0,1},{1,2},{2,3},{3,4},{4,5},{5,6},{6,7},{8,9},{9,10},{10,11},{11... | collective-permute-start | bytes 393224 | tf_op jit(solution)/shard_map/ppermute | solution.py:24
  60.0 1.3 collective-permute-start.5
  61.3 1.6 copy.46
  63.3 1.1 pad_maximum_fusion.2
  64.4 3.7 %fusion.52 = f32[8,128,512]{2,1,0:T(8,128)S(1)} fusion(bf16[8,512,128]{2,1,0:T(8,128)(2,1)S(1)} %bitcast.134, bf16[8,512,512]{2,1,0:T(8,128)(2,1)} %param.7), kind=kOutput, calls=%fused_computation.61 | convolution fusion | flops 536870912 | bytes 7340032 | tf_op jit(solution)/shard_map/bij,bjk->bik/dot_general | solution.py:43
  68.1 7.7 %fusion.35 = bf16[8,512,128]{1,2,0:T(8,128)(2,1)} fusion(bf16[1,8,512,512]{3,2,1,0:T(8,128)(2,1)} %param.6, bf16[8,512,128]{1,2,0:T(8,128)(2,1)S(1)} %copy.38, f32[8,128,512]{2,1,0:T(8,128)S(1)} %fusion.52, bf16[8,512,128]{2,1,0:T(8,128)(2,1)} %bitcast.141, bf16[8,512,512]{2,1,0:T(8,128)(2,1)} %param.8), kind=kOutput, calls=%fused_computation.28 | convolution fusion | flops 1076363264 | bytes 13631488 | tf_op jit(solution)/shard_map/bij,bjk->bik/dot_general | solution.py:49
  76.8 5.0 %collective-permute-start.6 = (bf16[512,128]{0,1:T(8,128)(2,1)S(1)}, bf16[512,128]{0,1:T(8,128)(2,1)S(1)}, u32[]{:S(2)}, u32[]{:S(2)}) collective-permute-start(bf16[512,128]{0,1:T(8,128)(2,1)S(1)} %get-tuple-element.8), channel_id=1, source_target_pairs={{0,1},{1,2},{2,3},{3,4},{4,5},{5,6},{6,7},{8,9},{9,10},{10,11},{11... | collective-permute-start | bytes 393224 | tf_op jit(solution)/shard_map/ppermute | solution.py:24
  81.8 1.5 collective-permute-start.7
  83.9 1.6 copy.51
  85.8 1.1 pad_maximum_fusion
  86.9 3.7 %fusion.53 = f32[8,128,512]{2,1,0:T(8,128)S(1)} fusion(bf16[8,512,128]{2,1,0:T(8,128)(2,1)S(1)} %bitcast.135, bf16[8,512,512]{2,1,0:T(8,128)(2,1)} %param.7), kind=kOutput, calls=%fused_computation.62 | convolution fusion | flops 536870912 | bytes 7340032 | tf_op jit(solution)/shard_map/bij,bjk->bik/dot_general | solution.py:43
  90.6 8.0 %multiply_bitcast_fusion = f32[8,512,128]{1,2,0:T(8,128)} fusion(bf16[1,8,512,512]{3,2,1,0:T(8,128)(2,1)} %param.6, bf16[8,512,128]{1,2,0:T(8,128)(2,1)S(1)} %copy.38, f32[8,128,512]{2,1,0:T(8,128)S(1)} %fusion.53, bf16[8,512,128]{2,1,0:T(8,128)(2,1)} %bitcast.131, bf16[8,512,512]{2,1,0:T(8,128)(2,1)} %param.8, f32[]{:T(128)} %bitcast.129), kind=kOutput, calls=%fused_computation.22 | convolution fusion | flops 1077411840 | bytes 14680068 | tf_op jit(solution)/shard_map/bij,bjk->bik/dot_general | solution.py:49
  98.6 2.9 %copy.56 = f32[8,512,128]{2,1,0:T(8,128)} copy(f32[8,512,128]{1,2,0:T(8,128)} %multiply_bitcast_fusion) | data formatting | bytes 4194304 | tf_op jit(solution)/shard_map/mul | solution.py:52
  101.5 71.9 %all-reduce.2.cloned.1.call-done = f32[4096,128]{1,0:T(8,128)} async-done(((f32[4096,128]{1,0:T(8,128)}), f32[4096,128]{1,0:T(8,128)}) %all-reduce.2.cloned.1.call-update) | async-done | bytes 2097168 | tf_op jit(solution)/shard_map/psum | solution.py:54
  173.4 5.7 %fusion.54 = f32[128,128]{1,0:T(8,128)S(1)} fusion(f32[4096,128]{1,0:T(8,128)} %all-reduce.2.cloned.1.call-done), kind=kOutput, calls=%fused_computation.63 | convolution fusion | flops 805306368 | bytes 2162688 | tf_op jit(solution)/shard_map/dot_general | solution.py:57
  179.1 15.0 %all-gather = f32[1024,128]{1,0:T(8,128)S(1)} all-gather(f32[128,128]{1,0:T(8,128)S(1)} %fusion.54), channel_id=2, replica_groups=mesh['pole'=4,'row'=8] {'row'}, dimensions={0}, use_global_device_ids=true | all-gather | bytes 589824 | tf_op jit(solution)/shard_map/all_gather | solution.py:11
  194.2 11.7 %cholesky.16 = f32[128,128]{1,0:T(8,128)S(1)} custom-call(f32[128,128]{1,0:T(8,128)S(1)} %fusion.48), custom_call_target="Cholesky" | custom-call | tf_op jit(solution)/shard_map/jit(cholesky)/cholesky | solution.py:60
  207.3 9.8 %custom-call.7 = f32[1,128,128]{1,2,0:T(8,128)S(1)} custom-call(f32[1,128,128]{2,1,0:T(8,128)S(1)} %fusion.46), custom_call_target="InvertDiagBlocksLowerTriangular" | custom-call | tf_op jit(solution)/shard_map/jit(_solve_triangular)/triangular_solve | solution.py:61
  217.1 2.4 %fusion.44 = f32[1024,128]{1,0:T(8,128)} fusion(f32[4096,128]{1,0:T(8,128)} %all-reduce.2.cloned.1.call-done, s32[]{:T(128)S(6)} %select_n.7, f32[1,128,128]{1,2,0:T(8,128)S(1)} %custom-call.7), kind=kOutput, calls=%fused_computation.39 | convolution fusion | flops 201326592 | bytes 1114116 | tf_op jit(solution)/shard_map/jit(_solve_triangular)/triangular_solve | solution.py:61
  (28 shorter events, 6.1 us)
Async XLA Ops:
  6.5 166.9 %all-reduce.2.cloned.1.call-start = ((), (), s32[]{:S(2)}) async-start(), calls=%async_computation | async-start | bytes 4194304 | tf_op jit(solution)/shard_map/psum | solution.py:54
  6.5 7.6 %copy-start = (bf16[4096,128]{1,0:T(8,128)(2,1)S(1)}, bf16[4096,128]{1,0:T(8,128)(2,1)}, u32[]{:S(2)}) copy-start(bf16[4096,128]{1,0:T(8,128)(2,1)} %param.5) | copy-start | bytes 3145732
  10.4 4.3 %collective-permute-start = (bf16[512,128]{1,0:T(8,128)(2,1)S(1)}, bf16[512,128]{1,0:T(8,128)(2,1)S(1)}, u32[]{:S(2)}, u32[]{:S(2)}) collective-permute-start(bf16[512,128]{1,0:T(8,128)(2,1)S(1)} %get-tuple-element.20), channel_id=1, source_target_pairs={{0,1},{1,2},{2,3},{3,4},{4,5},{5,6},{6,7},{8,9},{9,10},{10,11},{11... | collective-permute-start | bytes 393224 | tf_op jit(solution)/shard_map/ppermute | solution.py:24
  12.8 5.5 %collective-permute-start.1 = (bf16[512,128]{1,0:T(8,128)(2,1)S(1)}, bf16[512,128]{1,0:T(8,128)(2,1)}, u32[]{:S(2)}, u32[]{:S(2)}) collective-permute-start(bf16[512,128]{1,0:T(8,128)(2,1)S(1)} %get-tuple-element.19), channel_id=1, source_target_pairs={{1,0},{2,1},{3,2},{4,3},{5,4},{6,5},{7,6},{9,8},{10,9},{11,10},{12... | collective-permute-start | bytes 393224 | tf_op jit(solution)/shard_map/ppermute | solution.py:25
  32.7 8.4 %collective-permute-start.2 = (bf16[512,128]{0,1:T(8,128)(2,1)S(1)}, bf16[512,128]{0,1:T(8,128)(2,1)S(1)}, u32[]{:S(2)}, u32[]{:S(2)}) collective-permute-start(bf16[512,128]{0,1:T(8,128)(2,1)S(1)} %get-tuple-element.16), channel_id=1, source_target_pairs={{0,1},{1,2},{2,3},{3,4},{4,5},{5,6},{6,7},{8,9},{9,10},{10,11},{11... | collective-permute-start | bytes 393224 | tf_op jit(solution)/shard_map/ppermute | solution.py:24
  38.2 3.2 %collective-permute-start.3 = (bf16[512,128]{0,1:T(8,128)(2,1)S(1)}, bf16[512,128]{0,1:T(8,128)(2,1)S(1)}, u32[]{:S(2)}, u32[]{:S(2)}) collective-permute-start(bf16[512,128]{0,1:T(8,128)(2,1)S(1)} %get-tuple-element.15), channel_id=1, source_target_pairs={{1,0},{2,1},{3,2},{4,3},{5,4},{6,5},{7,6},{9,8},{10,9},{11,10},{12... | collective-permute-start | bytes 393224 | tf_op jit(solution)/shard_map/ppermute | solution.py:25
  55.0 7.9 %collective-permute-start.4 = (bf16[512,128]{0,1:T(8,128)(2,1)S(1)}, bf16[512,128]{0,1:T(8,128)(2,1)S(1)}, u32[]{:S(2)}, u32[]{:S(2)}) collective-permute-start(bf16[512,128]{0,1:T(8,128)(2,1)S(1)} %get-tuple-element.12), channel_id=1, source_target_pairs={{0,1},{1,2},{2,3},{3,4},{4,5},{5,6},{6,7},{8,9},{9,10},{10,11},{11... | collective-permute-start | bytes 393224 | tf_op jit(solution)/shard_map/ppermute | solution.py:24
  60.0 3.2 %collective-permute-start.5 = (bf16[512,128]{0,1:T(8,128)(2,1)S(1)}, bf16[512,128]{0,1:T(8,128)(2,1)S(1)}, u32[]{:S(2)}, u32[]{:S(2)}) collective-permute-start(bf16[512,128]{0,1:T(8,128)(2,1)S(1)} %get-tuple-element.11), channel_id=1, source_target_pairs={{1,0},{2,1},{3,2},{4,3},{5,4},{6,5},{7,6},{9,8},{10,9},{11,10},{12... | collective-permute-start | bytes 393224 | tf_op jit(solution)/shard_map/ppermute | solution.py:25
  76.8 8.7 %collective-permute-start.6 = (bf16[512,128]{0,1:T(8,128)(2,1)S(1)}, bf16[512,128]{0,1:T(8,128)(2,1)S(1)}, u32[]{:S(2)}, u32[]{:S(2)}) collective-permute-start(bf16[512,128]{0,1:T(8,128)(2,1)S(1)} %get-tuple-element.8), channel_id=1, source_target_pairs={{0,1},{1,2},{2,3},{3,4},{4,5},{5,6},{6,7},{8,9},{9,10},{10,11},{11... | collective-permute-start | bytes 393224 | tf_op jit(solution)/shard_map/ppermute | solution.py:24
  81.8 3.9 %collective-permute-start.7 = (bf16[512,128]{0,1:T(8,128)(2,1)S(1)}, bf16[512,128]{0,1:T(8,128)(2,1)S(1)}, u32[]{:S(2)}, u32[]{:S(2)}) collective-permute-start(bf16[512,128]{0,1:T(8,128)(2,1)S(1)} %get-tuple-element.7), channel_id=1, source_target_pairs={{1,0},{2,1},{3,2},{4,3},{5,4},{6,5},{7,6},{9,8},{10,9},{11,10},{12... | collective-permute-start | bytes 393224 | tf_op jit(solution)/shard_map/ppermute | solution.py:25
Sparse Core Ops, SparseCore 0:
  101.6 71.7 all-reduce.1
